TPU v7x, 32 devices: a whole 2x2x4 slice. The times are simulated.
32 devices in a mesh: rows: 16 (over z, x, core), split: 2 (over y).
Axes of the slice: x: 2, y: 2, z: 4, core: 2. Of those that a mesh axis runs over, the one named last changes fastest.
Arguments:
- embeddings: bfloat16 [8192, 768], P(('rows', 'split')), may hold values from -24 to 24
- cluster_id: int32 [8192], P(('rows', 'split')), may hold values from 0 to 127, as said below
- owner_map: int32 [128], replicated, may hold values from 0 to 15, as said below
Outputs:
- prune_score: float32 [8192], P(('rows', 'split'))
Inputs may be any that keep to these rules, and one draw needn't show every extreme that they name: `owner_map`: every group 0 to 15 holds exactly 8 clusters. `cluster_id`: within each aligned block of 256 rows (the rows of one device), no group holds more than 32 of the block's rows, and one group holds exactly 32; every group holds exactly 32 rows of some block. Every cluster holds two rows or more.
All inputs are finite; a program needn't handle non-finite values.
Results may differ from a plain program's by a relative error of at most 0.0005.
Values may be sent and summed in bfloat16 or wider, within the bound.
A program may use at most 64 MiB of HBM per device.

v0:
```python
import jax
import jax.numpy as jnp
from jax import lax
from jax.sharding import PartitionSpec as P

FLOOR_SCORE = -1e30


def block_logsumexp(queries, key_rows, allowed):
    score_scale = 1.0 / queries.shape[1] ** 0.5
    scores = (
        jnp.einsum("qd,kd->qk", queries, key_rows, preferred_element_type=jnp.float32) * score_scale
    )
    masked = jnp.where(allowed, scores, FLOOR_SCORE)
    highest = jnp.max(masked, axis=1)
    totals = jnp.sum(jnp.where(allowed, jnp.exp(masked - highest[:, None]), 0.0), axis=1)
    return (highest, totals)


def merge_pair(earlier_pair, later_pair):
    highest = jnp.maximum(earlier_pair[0], later_pair[0])
    totals = later_pair[1] * jnp.exp(later_pair[0] - highest)
    return (highest, totals)


def cluster_means(density, member_ids, clusters_all):
    present = member_ids >= 0
    segment = jnp.where(present, member_ids, clusters_all)
    sum_density = jax.ops.segment_sum(jnp.where(present, density, 0.0), segment, clusters_all + 1)[
        :clusters_all
    ]
    counts = jax.ops.segment_sum(present.astype(jnp.float32), segment, clusters_all + 1)[
        :clusters_all
    ]
    return (sum_density, counts)


def on_device(embeddings, cluster_id, owner_map):
    rows_here = embeddings.shape[0]
    width = embeddings.shape[1]
    clusters_all = owner_map.shape[0]
    owners_count = lax.axis_size("rows")
    capacity = 2 * rows_here // owners_count
    slot_count = owners_count * capacity
    cluster_range = jnp.arange(clusters_all, dtype=jnp.int32)
    table_hit = cluster_id[:, None] == cluster_range[None, :]
    owner_of = jnp.sum(jnp.where(table_hit, owner_map[None, :], 0), axis=1)
    same_owner = owner_of[:, None] == owner_of[None, :]
    earlier = jnp.arange(rows_here)[None, :] < jnp.arange(rows_here)[:, None]
    ranking = jnp.sum(same_owner & earlier, axis=1)
    slot_index = owner_of * capacity + ranking
    placed = jnp.arange(slot_count, dtype=jnp.int32)[:, None] == slot_index[None, :]
    outgoing = jnp.dot(
        placed.astype(jnp.bfloat16), embeddings, preferred_element_type=jnp.float32
    ).astype(jnp.bfloat16)
    out_ids = jnp.sum(jnp.where(placed, cluster_id[None, :] + 1, 0), axis=1) - 1
    arrived, arrived_ids = (
        lax.all_to_all(
            outgoing.reshape(owners_count, capacity, width),
            "rows",
            split_axis=0,
            concat_axis=0,
            tiled=True,
        ),
        lax.all_to_all(
            out_ids.reshape(owners_count, capacity), "rows", split_axis=0, concat_axis=0, tiled=True
        ),
    )
    key_rows = arrived.reshape(slot_count, width)
    key_ids = arrived_ids.reshape(slot_count)
    piece_index = lax.axis_index("split")
    my_start = piece_index * slot_count
    positions = my_start + jnp.arange(slot_count, dtype=jnp.int32)
    initial = (
        jnp.full((slot_count,), FLOOR_SCORE, jnp.float32),
        jnp.zeros((slot_count,), jnp.float32),
    )
    portion_rows = lax.all_gather(key_rows, "split", axis=0, tiled=True)
    portion_ids = lax.all_gather(key_ids, "split", axis=0, tiled=True)
    length = portion_ids.shape[0]
    key_positions = jnp.arange(length, dtype=jnp.int32)
    allowed = (
        (portion_ids[None, :] >= 0)
        & (portion_ids[None, :] == key_ids[:, None])
        & (positions[:, None] != key_positions[None, :])
    )
    highest, totals = merge_pair(initial, block_logsumexp(key_rows, portion_rows, allowed))
    density = highest + jnp.log(totals)
    sum_density, counts = cluster_means(density, key_ids, clusters_all)
    sum_density, counts = lax.psum((sum_density, counts), "split")
    cluster_mean = sum_density / jnp.maximum(counts, 1.0)
    row_hit = key_ids[:, None] == cluster_range[None, :]
    row_mean = jnp.sum(jnp.where(row_hit, cluster_mean[None, :], 0.0), axis=1)
    slot_score = jnp.where(key_ids >= 0, density - row_mean, 0.0)
    returned = lax.all_to_all(
        slot_score.reshape(owners_count, capacity), "rows", split_axis=0, concat_axis=0, tiled=True
    )
    returned_flat = returned.reshape(slot_count)
    return jnp.sum(jnp.where(placed, returned_flat[:, None], 0.0), axis=0)


def solution(mesh):
    placed = (P(("rows", "split"), None), P(("rows", "split")), P())
    return jax.shard_map(
        on_device, mesh=mesh, in_specs=placed, out_specs=P(("rows", "split")), check_vma=False
    )
```

profile of v0, /device:TPU:0, one launch (start us, length us, event | category | flops | bytes accessed | tf_op | source)
XLA Modules:
  0.0 97.4 jit_solution(236340904709516073)
XLA Ops:
  6.5 0.0 copy-start
  6.5 0.0 all-gather.3.cloned.1.call-start
  6.5 0.9 select_reduce_fusion.4
  7.5 0.2 convert_reduce_fusion
  7.6 0.7 multiply_add_fusion
  8.3 0.0 copy-done
  8.3 0.4 convolution_convert_fusion
  8.7 27.4 %all_to_all.17 = bf16[16,32,768]{2,1,0:T(8,128)(2,1)} all-to-all(bf16[16,32,768]{2,1,0:T(8,128)(2,1)S(1)} %bitcast.10), channel_id=1, replica_groups=mesh['rows'=16,'split'=2] {'rows'}, dimensions={0} | all-to-all | bytes 1572864 | tf_op jit(solution)/shard_map/all_to_all | solution.py:58
  36.1 0.0 all-gather.3.cloned.1.call-update
  36.2 0.1 select_reduce_fusion.2
  36.3 0.7 sub.39
  37.0 3.9 %all-to-all-start = ((s32[16,1,32]{2,1,0:T(1,128)}), s32[16,1,32]{2,1,0:T(1,128)S(1)}, u32[]{:S(2)}, u32[]{:S(2)}) async-start(s32[16,1,32]{2,1,0:T(1,128)} %sub.39), calls=%async_computation | async-start | bytes 16384 | tf_op jit(solution)/shard_map/all_to_all | solution.py:65
  41.0 6.4 %all-to-all-done = s32[16,1,32]{2,1,0:T(1,128)S(1)} async-done(((s32[16,1,32]{2,1,0:T(1,128)}), s32[16,1,32]{2,1,0:T(1,128)S(1)}, u32[]{:S(2)}, u32[]{:S(2)}) %all-to-all-start) | async-done | bytes 2080 | tf_op jit(solution)/shard_map/all_to_all | solution.py:65
  47.4 0.1 reshape.127
  47.5 0.1 reshape.130
  47.5 0.5 broadcast.91
  48.0 0.7 reduce.10
  48.7 0.1 reshape.147
  48.8 4.1 %scatter_custom_fusion.1 = f32[129]{0:T(256)S(1)} fusion(s32[512]{0:T(512)S(1)} %bitcast.16, f32[512]{0:T(512)S(1)} %get-tuple-element.7, f32[]{:T(128)} %constant.6.clone.1), kind=kCustom, calls=%fused_computation.38 | custom fusion | flops 512 | bytes 520 | tf_op jit(solution)/shard_map/scatter-add | solution.py:32
  52.9 0.0 copy-start.1
  52.9 4.5 %all-gather = s32[2,1,512]{2,1,0:T(1,128)S(1)} all-gather(s32[1,1,512]{2,1,0:T(1,128)S(1)} %reshape.147), channel_id=1, replica_groups=mesh['rows'=16,'split'=2] {'split'}, dimensions={0}, use_global_device_ids=true | all-gather | bytes 6144 | tf_op jit(solution)/shard_map/all_gather | solution.py:79
  57.5 5.4 %all-gather.3.cloned.1.call-done = bf16[1024,768]{1,0:T(8,128)(2,1)} async-done(((bf16[512,768]{1,0:T(8,128)(2,1)}), bf16[1024,768]{1,0:T(8,128)(2,1)}) %all-gather.3.cloned.1.call-update) | async-done | bytes 1572880 | tf_op jit(solution)/shard_map/all_gather | solution.py:78
  62.9 3.1 %fusion.1 = (f32[512]{0:T(512)S(1)}, f32[512,1024]{1,0:T(8,128)S(1)}) fusion(s32[512]{0:T(512)S(1)} %iota_add_fusion, s32[1024]{0:T(1024)S(1)} %bitcast.14, s32[512]{0:T(512)S(1)} %reshape.127, pred[1024]{0:T(1024)(128)(4,1)S(1)} %broadcast_compare_fusion, bf16[512,768]{1,0:T(8,128)(2,1)} %bitcast.9, bf16[1024,768]{1,0:T(8,128)(2,1)} %all-gather.3.cloned.1.call-done), kind=kOutput, calls=%fused_computation.6 | convolution fusion | flops 808975872 | bytes 4467712 | tf_op jit(solution)/shard_map/qd,kd->qk/dot_general | solution.py:12
  65.9 0.0 copy-done.1
  65.9 0.0 slice-start
  65.9 0.1 reduce_max.12
  66.0 1.2 %select_reduce_fusion = f32[512]{0:T(512)S(1)} fusion(f32[512,1024]{1,0:T(8,128)S(1)} %get-tuple-element.10, f32[512]{0:T(512)S(1)} %get-tuple-element.9, s32[512]{0:T(512)S(1)} %iota_add_fusion, s32[1024]{0:T(1024)S(1)} %bitcast.15, s32[512]{0:T(512)S(1)} %reshape.127, pred[1024]{0:T(1024)(128)(4,1)S(1)} %broadcast_compare_fusion), kind=kLoop, calls=%fused_computation.2 | loop fusion | flops 4718080 | bytes 2110464 | tf_op jit(solution)/shard_map/reduce_sum | solution.py:16
  67.2 0.1 reduce_sum.62
  67.3 4.1 %scatter_custom_fusion = f32[129]{0:T(256)S(1)} fusion(s32[512]{0:T(512)S(1)} %bitcast.17, f32[512]{0:T(512)S(1)} %fusion.10, f32[]{:T(128)} %constant.6.clone.1), kind=kCustom, calls=%fused_computation.40 | custom fusion | flops 512 | bytes 520 | tf_op jit(solution)/shard_map/scatter-add | solution.py:29
  71.4 0.0 slice-done
  71.4 4.9 %all-reduce = (f32[128]{0:T(128)S(1)}, f32[128]{0:T(128)S(1)}) all-reduce(f32[128]{0:T(128)S(1)} %slice.6, f32[128]{0:T(128)S(1)} %slice-done), channel_id=1, replica_groups=mesh['rows'=16,'split'=2] {'split'}, use_global_device_ids=true, to_apply=%region_6.7 | all-reduce | flops 256 | bytes 2048 | tf_op jit(solution)/shard_map/psum | solution.py:90
  76.4 0.2 select_reduce_fusion.3
  76.6 0.1 reduce_sum.64
  76.7 11.9 %all_to_all.18 = f32[16,1,32]{2,1,0:T(1,128)S(1)} all-to-all(f32[16,1,32]{2,1,0:T(1,128)S(1)} %compare_select_fusion), channel_id=1, replica_groups=mesh['rows'=16,'split'=2] {'rows'}, dimensions={0} | all-to-all | bytes 4096 | tf_op jit(solution)/shard_map/all_to_all | solution.py:95
  88.6 0.5 broadcast.92
  89.1 0.7 reduce.11
  89.8 0.1 broadcast_in_dim.105
  89.9 0.7 select_reduce_fusion.1
  (9 shorter events, 0.1 us)
Async XLA Ops:
  6.5 1.8 %copy-start = (bf16[256,768]{1,0:T(8,128)(2,1)S(1)}, bf16[256,768]{1,0:T(8,128)(2,1)}, u32[]{:S(2)}) copy-start(bf16[256,768]{1,0:T(8,128)(2,1)} %param.3) | copy-start | bytes 1179652
  6.5 56.3 %all-gather.3.cloned.1.call-start = ((), (), s32[]{:S(2)}) async-start(), calls=%async_computation.3 | async-start | bytes 2359296 | tf_op jit(solution)/shard_map/all_gather | solution.py:78
  37.0 10.4 %all-to-all-start = ((s32[16,1,32]{2,1,0:T(1,128)}), s32[16,1,32]{2,1,0:T(1,128)S(1)}, u32[]{:S(2)}, u32[]{:S(2)}) async-start(s32[16,1,32]{2,1,0:T(1,128)} %sub.39), calls=%async_computation | async-start | bytes 16384 | tf_op jit(solution)/shard_map/all_to_all | solution.py:65
  52.9 13.0 %copy-start.1 = (f32[129]{0:T(256)}, f32[129]{0:T(256)S(1)}, u32[]{:S(2)}) copy-start(f32[129]{0:T(256)S(1)} %scatter_custom_fusion.1) | copy-start | bytes 1552
  65.9 5.5 %slice-start = ((f32[129]{0:T(256)}), f32[128]{0:T(128)S(1)}, s32[]{:S(2)}) async-start(f32[129]{0:T(256)} %copy-done.1), calls=%async_computation.4 | async-start | bytes 1024 | tf_op jit(solution)/shard_map/slice | solution.py:32
Sparse Core Ops, SparseCore 0:
  36.3 26.5 all-gather.2
where the time goes:
time: 97.8 us; the launch traced here: 97.4 us
  blocking collectives  48.7 us (50%)
  other arithmetic  13.7 us (14%)
  between operations  13.5 us (14%)
  waiting for transfers between devices  11.8 us (12%)
  starting transfers between devices  3.94 us (4%)
  matrix products  3.43 us (4%)
  local copies, waits for them, and re-layouts  2.3 us (2%)
    all_to_all x1, blocking collectives, on_device(): lax.all_to_all(outgoing.reshape(owners_count, capacity, width), 'rows', s...  27.4 us
    all_to_all x1, blocking collectives, on_device(): lax.all_to_all(slot_score.reshape(owners_count, capacity), 'rows', split_...  11.9 us
    all_to_all x1, waiting for transfers between devices, on_device(): lax.all_to_all(out_ids.reshape(owners_count, capacity), 'rows', split_axi...  6.42 us
    all_gather x1, waiting for transfers between devices, on_device(): portion_rows = lax.all_gather(key_rows, 'split', axis=0, tiled=True)  5.4 us
    psum x1, blocking collectives, on_device(): sum_density, counts = lax.psum((sum_density, counts), 'split')  4.93 us
    all_gather x1, blocking collectives, on_device(): portion_ids = lax.all_gather(key_ids, 'split', axis=0, tiled=True)  4.54 us
    scatter-add x1, other arithmetic, cluster_means(): jax.ops.segment_sum(jnp.where(present, density, 0.0), segment, clusters_a...  4.09 us
    scatter-add x1, other arithmetic, cluster_means(): jax.ops.segment_sum(present.astype(jnp.float32), segment, clusters_all + 1)  4.09 us
  transfers between devices with their start and end apart: 2, of which 2 were waited for; matrix products, arithmetic and copies ran while one was open for 7% of the time, Pallas kernels for 0%

commit v1 on v0

v1 whole, which is shorter than its diff:
```python
import functools

import jax
import jax.numpy as jnp
from jax import lax
from jax.experimental import pallas as pl
from jax.experimental.pallas import tpu as pltpu
from jax.sharding import PartitionSpec as P

FLOOR_SCORE = -1e30
LANES = 128
KEY_CHUNK = 256
MESH = pl.DeviceIdType.MESH
F32 = jnp.float32
BF16 = jnp.bfloat16


def iota(shape, dim):
    return lax.broadcasted_iota(jnp.int32, shape, dim)


def one_hot(hit, dtype=BF16):
    return jnp.where(hit, 1.0, 0.0).astype(dtype)


def dot(a, b, dims=((1,), (0,)), precision=None):
    return lax.dot_general(a, b, (dims, ((), ())), preferred_element_type=F32, precision=precision)


def column_to_row(column):
    blocks = [
        jnp.transpose(jnp.broadcast_to(column[at : at + LANES], (LANES, LANES)))[0:1]
        for at in range(0, column.shape[0], LANES)
    ]
    return jnp.concatenate(blocks, axis=1)


def kernel(
    groups, parts, local_clusters,
    emb_ref, cid_ref, owner_ref, out_ref,
    outgoing, out_ids, keys, key_ids, id_rows, id_cols, scores, sums, result, returned,
    send_sem, recv_sem, id_send, id_recv, fwd_send, fwd_recv, idf_send, idf_recv,
    sum_send, sum_recv, ret_send, ret_recv, local_sem,
):
    rows_here, width = emb_ref.shape
    clusters_all = owner_ref.shape[1]
    cap = outgoing.shape[1]
    per_row = LANES // cap
    slots = groups * cap
    lane_rows = slots // LANES
    r, s = lax.axis_index("rows"), lax.axis_index("split")
    me = (r // parts) * parts + s
    part = r % parts

    def device(group, piece):
        return ((group // parts) * parts + piece, group % parts)

    def step_offset(t):
        half = (t + 1) // 2
        return groups // 2 + half - 2 * half * ((t + 1) % 2)

    def peer_out(t):
        return (me + step_offset(t)) % groups

    def peer_in(t):
        return (me + groups - step_offset(t)) % groups

    def sibling(d):
        return (part + d) % parts

    barrier = pltpu.get_barrier_semaphore()

    @pl.loop(0, groups - 1)
    def _(t):
        pl.semaphore_signal(barrier, inc=1, device_id=device(peer_out(t), part), device_id_type=MESH)

    for d in range(1, parts):
        pl.semaphore_signal(barrier, inc=1, device_id=device(me, sibling(d)), device_id_type=MESH)

    cid = cid_ref[...]
    cluster_hit = one_hot(iota((clusters_all, rows_here), 0) == cid)
    owner_cl = iota((groups, clusters_all), 0) == owner_ref[...]
    owner_cl_hot = one_hot(owner_cl)
    before_cl = one_hot(iota((clusters_all, clusters_all), 0) < iota((clusters_all, clusters_all), 1))
    local_rank = dot(owner_cl_hot, before_cl)
    label_cl = jnp.where(owner_cl, local_rank + 1.0, 0.0).astype(BF16)
    labels = dot(label_cl, cluster_hit)
    owner_hot = jnp.where(labels > 0.5, 1.0, 0.0)
    before = one_hot(iota((rows_here, rows_here), 0) < iota((rows_here, rows_here), 1))
    prefix = dot(owner_hot.astype(BF16), before)
    rank = jnp.sum(owner_hot * prefix, axis=0, keepdims=True).astype(jnp.int32)
    lane_hit = one_hot(iota((LANES, rows_here), 0) == rank + (me % per_row) * cap, F32)
    id_block = dot(labels.astype(BF16), lane_hit.astype(BF16), ((1,), (1,)))
    for g in range(groups):
        out_ids[g] = id_block[g : g + 1]
    rank_hot = one_hot(iota((cap, rows_here), 0) == rank, F32)
    emb = emb_ref[...]
    per_step = max(1, 256 // cap)
    for g0 in range(0, groups, per_step):
        placed = jnp.concatenate(
            [(rank_hot * owner_hot[g : g + 1]).astype(BF16) for g in range(g0, min(g0 + per_step, groups))], axis=0
        )
        outgoing[g0 : g0 + per_step] = dot(placed, emb).astype(BF16).reshape(per_step, cap, width)

    def row_copy(to, frm):
        return pltpu.make_async_remote_copy(
            src_ref=outgoing.at[to], dst_ref=keys.at[part, me],
            send_sem=send_sem.at[to], recv_sem=recv_sem.at[frm],
            device_id=device(to, part), device_id_type=MESH,
        )

    def id_copy(to, frm):
        return pltpu.make_async_remote_copy(
            src_ref=out_ids.at[to], dst_ref=key_ids.at[part, me],
            send_sem=id_send.at[to], recv_sem=id_recv.at[frm],
            device_id=device(to, part), device_id_type=MESH,
        )

    def forward(q, piece, d, home):
        return pltpu.make_async_remote_copy(
            src_ref=keys.at[home, q], dst_ref=keys.at[home, q],
            send_sem=fwd_send.at[d, q], recv_sem=fwd_recv.at[home, q],
            device_id=device(me, piece), device_id_type=MESH,
        )

    def forward_ids(piece, d, home):
        return pltpu.make_async_remote_copy(
            src_ref=key_ids.at[home], dst_ref=key_ids.at[home],
            send_sem=idf_send.at[d], recv_sem=idf_recv.at[home],
            device_id=device(me, piece), device_id_type=MESH,
        )

    pl.semaphore_wait(barrier, groups + parts - 2)

    @pl.loop(0, groups - 1)
    def _(t):
        to = peer_out(t)
        id_copy(to, me).start()
        row_copy(to, me).start()

    own_rows = pltpu.make_async_copy(outgoing.at[me], keys.at[part, me], local_sem.at[0])
    own_ids = pltpu.make_async_copy(out_ids.at[me], key_ids.at[part, me], local_sem.at[1])
    own_rows.start()
    own_ids.start()
    own_rows.wait()
    own_ids.wait()
    for d in range(1, parts):
        forward(me, sibling(d), d, part).start()

    @pl.loop(0, groups - 1)
    def _(t):
        q = peer_in(t)
        row_copy(q, q).wait_recv()
        for d in range(1, parts):
            forward(q, sibling(d), d, part).start()

    @pl.loop(0, groups - 1)
    def _(t):
        q = peer_in(t)
        id_copy(q, q).wait_recv()

    for d in range(1, parts):
        forward_ids(sibling(d), d, part).start()
    for d in range(1, parts):
        home = sibling(d)
        forward_ids(home, d, home).wait_recv()

    for piece in range(parts):
        for l in range(lane_rows):
            row = key_ids[piece, l * per_row]
            for j in range(1, per_row):
                row = row + key_ids[piece, l * per_row + j]
            id_rows[piece, l] = row
    query_rows = []
    for l in range(lane_rows):
        row = id_rows[part, l]
        query_rows.append(row)
        id_cols[l * LANES : (l + 1) * LANES] = jnp.transpose(jnp.broadcast_to(row, (LANES, LANES)))

    for d in range(1, parts):
        home = sibling(d)

        @pl.loop(0, groups)
        def _(q):
            forward(q, home, d, home).wait_recv()

    scale = 1.0 / width**0.5
    chunk_groups = KEY_CHUNK // cap
    chunk_lanes = KEY_CHUNK // LANES
    per_piece = groups // chunk_groups
    n_chunks = parts * per_piece

    queries = keys[part].reshape(slots, width)
    id_col = jnp.concatenate([id_cols[...]] * chunk_lanes, axis=1)
    gap = iota((slots, KEY_CHUNK), 0) - iota((slots, KEY_CHUNK), 1)

    def score_chunk(j, high):
        piece, at = j // per_piece, j % per_piece
        block = keys[piece, pl.ds(at * chunk_groups, chunk_groups)].reshape(KEY_CHUNK, width)
        raw = dot(queries, block, ((1,), (1,))) * scale
        id_row = jnp.concatenate([id_rows[piece, at * chunk_lanes + i] for i in range(chunk_lanes)], axis=1)
        own_gap = (piece - part) * slots + at * KEY_CHUNK
        masked = jnp.where((id_col == id_row) & (gap != own_gap), raw, FLOOR_SCORE)
        scores[j] = masked
        folded = masked[:, :LANES]
        for i in range(1, chunk_lanes):
            folded = jnp.maximum(folded, masked[:, i * LANES : (i + 1) * LANES])
        return jnp.maximum(high, folded)

    high = lax.fori_loop(
        0, n_chunks, score_chunk, jnp.full((slots, LANES), FLOOR_SCORE, F32), unroll=n_chunks <= 4
    )
    highest = jnp.max(high, axis=1, keepdims=True)

    def sum_chunk(j, total):
        value = jnp.exp(scores[j] - highest)
        for i in range(chunk_lanes):
            total = total + value[:, i * LANES : (i + 1) * LANES]
        return total

    total = lax.fori_loop(0, n_chunks, sum_chunk, jnp.zeros((slots, LANES), F32), unroll=n_chunks <= 4)
    density = column_to_row(highest + jnp.log(jnp.sum(total, axis=1, keepdims=True)))
    labels_row = jnp.concatenate(query_rows, axis=1)
    member = labels_row == (iota((local_clusters, slots), 0) + 1).astype(F32)
    part_sum = jnp.sum(jnp.where(member, density, 0.0), axis=1, keepdims=True)
    part_count = jnp.sum(jnp.where(member, 1.0, 0.0), axis=1, keepdims=True)
    sums[part] = jnp.where(iota((local_clusters, LANES), 1) == 0, part_sum, part_count)

    def sum_copy(piece, d, home):
        return pltpu.make_async_remote_copy(
            src_ref=sums.at[home], dst_ref=sums.at[home],
            send_sem=sum_send.at[d], recv_sem=sum_recv.at[home],
            device_id=device(me, piece), device_id_type=MESH,
        )

    for d in range(1, parts):
        sum_copy(sibling(d), d, part).start()
    for d in range(1, parts):
        home = sibling(d)
        sum_copy(home, d, home).wait_recv()
    both = sums[0]
    for piece in range(1, parts):
        both = both + sums[piece]
    mean = both[:, 0:1] / jnp.maximum(both[:, 1:2], 1.0)
    row_mean = jnp.sum(jnp.where(member, mean, 0.0), axis=0, keepdims=True)
    final = jnp.where(labels_row > 0.5, density - row_mean, 0.0)
    for l in range(lane_rows):
        result[l] = final[:, l * LANES : (l + 1) * LANES]

    def ret_copy(to, frm):
        return pltpu.make_async_remote_copy(
            src_ref=result.at[to // per_row], dst_ref=returned.at[me],
            send_sem=ret_send.at[to], recv_sem=ret_recv.at[frm],
            device_id=device(to, part), device_id_type=MESH,
        )

    @pl.loop(0, groups - 1)
    def _(t):
        ret_copy(peer_out(t), me).start()

    own_ret = pltpu.make_async_copy(result.at[me // per_row], returned.at[me], local_sem.at[2])
    own_ret.start()
    own_ret.wait()

    @pl.loop(0, groups - 1)
    def _(t):
        q = peer_in(t)
        id_copy(q, q).wait_send()
        row_copy(q, q).wait_send()

    for d in range(1, parts):
        forward_ids(sibling(d), d, part).wait_send()
        sum_copy(sibling(d), d, part).wait_send()

        @pl.loop(0, groups)
        def _(q):
            forward(q, sibling(d), d, part).wait_send()

    @pl.loop(0, groups - 1)
    def _(t):
        q = peer_in(t)
        ret_copy(q, q).wait_recv()

    back = jnp.concatenate([returned[g] for g in range(groups)], axis=0)
    picked = dot(back, lane_hit, precision=lax.Precision.HIGHEST)
    out_ref[...] = jnp.sum(owner_hot * picked, axis=0, keepdims=True)

    @pl.loop(0, groups - 1)
    def _(t):
        q = peer_in(t)
        ret_copy(q, q).wait_send()


def on_device(embeddings, cluster_id, owner_map):
    rows_here, width = embeddings.shape
    clusters_all = owner_map.shape[0]
    groups = lax.axis_size("rows")
    parts = lax.axis_size("split")
    cap = 2 * rows_here // groups
    slots = groups * cap
    lane_rows = slots // LANES
    local_clusters = clusters_all // groups
    dma = pltpu.SemaphoreType.DMA
    vmem = pl.BlockSpec(memory_space=pltpu.VMEM)
    out = pl.pallas_call(
        functools.partial(kernel, groups, parts, local_clusters),
        out_shape=jax.ShapeDtypeStruct((1, rows_here), F32),
        in_specs=[vmem] * 3,
        out_specs=vmem,
        scratch_shapes=[
            pltpu.VMEM((groups, cap, width), BF16),
            pltpu.VMEM((groups, 1, LANES), F32),
            pltpu.VMEM((parts, groups, cap, width), BF16),
            pltpu.VMEM((parts, groups, 1, LANES), F32),
            pltpu.VMEM((parts, lane_rows, 1, LANES), F32),
            pltpu.VMEM((slots, LANES), F32),
            pltpu.VMEM((parts * slots // KEY_CHUNK, slots, KEY_CHUNK), F32),
            pltpu.VMEM((parts, local_clusters, LANES), F32),
            pltpu.VMEM((lane_rows, 1, LANES), F32),
            pltpu.VMEM((groups, 1, LANES), F32),
            dma((groups,)), dma((groups,)), dma((groups,)), dma((groups,)),
            dma((parts, groups)), dma((parts, groups)), dma((parts,)), dma((parts,)),
            dma((parts,)), dma((parts,)), dma((groups,)), dma((groups,)), dma((3,)),
        ],
        compiler_params=pltpu.CompilerParams(
            collective_id=0, has_side_effects=True, vmem_limit_bytes=60 * 1024 * 1024
        ),
        name="soft_neighbour",
    )(embeddings, cluster_id.reshape(1, rows_here), owner_map.reshape(1, clusters_all))
    return out.reshape(rows_here)


def solution(mesh):
    placed = (P(("rows", "split"), None), P(("rows", "split")), P())
    return jax.shard_map(
        on_device, mesh=mesh, in_specs=placed, out_specs=P(("rows", "split")), check_vma=False
    )
```

time: 97.8 us -> 39.6 us (0.40)
  blocking collectives: 48.7 us -> 0 us
  Pallas kernels: 0 us -> 38.2 us
  other arithmetic: 13.7 us -> 0 us
  between operations: 13.5 us -> 0.02 us
  waiting for transfers between devices: 11.8 us -> 0 us
  starting transfers between devices: 3.94 us -> 0 us
  matrix products: 3.43 us -> 0 us
  local copies, waits for them, and re-layouts: 2.3 us -> 1.22 us
    all_to_all x2 -> x0, blocking collectives: 39.3 us -> none  [the longest x1 27.4 us: on_device(): lax.all_to_all(outgoing.reshape(owners_count, capacity, width), 'rows', s...]
    pallas_call x0 -> x1, Pallas kernels: none -> 38.2 us  [on_device(): pl.pallas_call(functools.partial(kernel, groups, parts, local_clusters),...]
    scatter-add x2 -> x0, other arithmetic: 8.18 us -> none  [the longest x1 4.09 us: cluster_means(): jax.ops.segment_sum(jnp.where(present, density, 0.0), segment, clusters_a...]
    all_to_all x1 -> x0, waiting for transfers between devices: 6.42 us -> none  [on_device(): lax.all_to_all(out_ids.reshape(owners_count, capacity), 'rows', split_axi...]
    all_gather x1 -> x0, waiting for transfers between devices: 5.4 us -> none  [on_device(): portion_rows = lax.all_gather(key_rows, 'split', axis=0, tiled=True)]
    psum x1 -> x0, blocking collectives: 4.93 us -> none  [on_device(): sum_density, counts = lax.psum((sum_density, counts), 'split')]
    all_gather x1 -> x0, blocking collectives: 4.54 us -> none  [on_device(): portion_ids = lax.all_gather(key_ids, 'split', axis=0, tiled=True)]
    all_to_all x1 -> x0, starting transfers between devices: 3.93 us -> none  [on_device(): lax.all_to_all(out_ids.reshape(owners_count, capacity), 'rows', split_axi...]
  transfers between devices with their start and end apart: 2 -> 0, of which waited for: 2 -> 0; matrix products, arithmetic and copies ran while one was open for 7% -> 0% of each run, Pallas kernels for 0% -> 0%
where the time goes in v1:
time: 39.6 us; the launch traced here: 39.5 us
  Pallas kernels  38.2 us (96%)
  local copies, waits for them, and re-layouts  1.22 us (3%)
    pallas_call x1, Pallas kernels, on_device(): pl.pallas_call(functools.partial(kernel, groups, parts, local_clusters),...  38.2 us
    unnamed x3, local copies, waits for them, and re-layouts  1.22 us

profile of v1, /device:TPU:0, one launch (start us, length us, event | category | flops | bytes accessed | tf_op | source)
XLA Modules:
  0.0 39.5 jit_solution(9263718439354178239)
XLA Ops:
  0.0 38.2 %soft_neighbour.1 = f32[1,256]{1,0:T(1,128)} custom-call(bf16[256,768]{1,0:T(8,128)(2,1)} %emb_ref.1, s32[1,256]{1,0:T(1,128)} %bitcast.4, s32[1,128]{1,0:T(1,128)} %bitcast.5), custom_call_target="tpu_custom_call" | custom-call | tf_op jit(solution)/shard_map/soft_neighbour/pallas_call | solution.py:305
  38.3 0.0 copy-start
  38.3 0.7 %copy-done = f32[1,256]{1,0:T(1,128)S(1)} copy-done((f32[1,256]{1,0:T(1,128)S(1)}, f32[1,256]{1,0:T(1,128)}, u32[]{:S(2)}) %copy-start) | copy-done | bytes 1048
  38.9 0.6 %copy.5 = f32[256]{0:T(256)} copy(f32[256]{0:T(256)S(1)} %bitcast.3) | data formatting | bytes 2048
Async XLA Ops:
  38.3 0.7 %copy-start = (f32[1,256]{1,0:T(1,128)S(1)}, f32[1,256]{1,0:T(1,128)}, u32[]{:S(2)}) copy-start(f32[1,256]{1,0:T(1,128)} %soft_neighbour.1) | copy-start | bytes 3076

commit v2 on v1

--- a/solution.py
+++ b/solution.py
@@ -10,6 +10,7 @@
 FLOOR_SCORE = -1e30
 LANES = 128
 KEY_CHUNK = 256
+PLANE = 4
 MESH = pl.DeviceIdType.MESH
 F32 = jnp.float32
 BF16 = jnp.bfloat16
@@ -40,7 +41,7 @@
     emb_ref, cid_ref, owner_ref, out_ref,
     outgoing, out_ids, keys, key_ids, id_rows, id_cols, scores, sums, result, returned,
     send_sem, recv_sem, id_send, id_recv, fwd_send, fwd_recv, idf_send, idf_recv,
-    sum_send, sum_recv, ret_send, ret_recv, local_sem,
+    sum_send, sum_recv, ret_send, ret_recv, local_sem, diag_sem, up_sem, down_sem,
 ):
     rows_here, width = emb_ref.shape
     clusters_all = owner_ref.shape[1]
@@ -70,10 +71,24 @@
 
     barrier = pltpu.get_barrier_semaphore()
 
-    @pl.loop(0, groups - 1)
-    def _(t):
-        pl.semaphore_signal(barrier, inc=1, device_id=device(peer_out(t), part), device_id_type=MESH)
-
+    levels = groups // PLANE
+    z, a, b = me // PLANE, me // 2 % 2, me % 2
+
+    def group_at(level, da, db):
+        return level * PLANE + (a + da) % 2 * 2 + (b + db) % 2
+
+    def tell(semaphore, group):
+        pl.semaphore_signal(semaphore, inc=1, device_id=device(group, part), device_id_type=MESH)
+
+    def beside(level, action):
+        @pl.when((level >= 0) & (level < levels))
+        def _():
+            action()
+
+    tell(barrier, group_at(z, 1, 0))
+    tell(barrier, group_at(z, 0, 1))
+    beside(z - 1, lambda: tell(barrier, group_at(z - 1, 0, 0)))
+    beside(z + 1, lambda: tell(barrier, group_at(z + 1, 0, 0)))
     for d in range(1, parts):
         pl.semaphore_signal(barrier, inc=1, device_id=device(me, sibling(d)), device_id_type=MESH)
 
@@ -130,13 +145,38 @@
             device_id=device(me, piece), device_id_type=MESH,
         )
 
-    pl.semaphore_wait(barrier, groups + parts - 2)
-
-    @pl.loop(0, groups - 1)
-    def _(t):
-        to = peer_out(t)
-        id_copy(to, me).start()
-        row_copy(to, me).start()
+    def send(group):
+        id_copy(group, me).start()
+        row_copy(group, me).start()
+
+    pl.semaphore_wait(
+        barrier, parts + 1 + jnp.where(z > 0, 1, 0) + jnp.where(z < levels - 1, 1, 0)
+    )
+    beside(z - 1, lambda: send(group_at(z - 1, 0, 0)))
+    beside(z + 1, lambda: send(group_at(z + 1, 0, 0)))
+    tell(diag_sem, group_at(z, 1, 0))
+    send(group_at(z, 1, 0))
+    send(group_at(z, 0, 1))
+    pl.semaphore_wait(diag_sem, 1)
+    beside(z + 1, lambda: tell(up_sem.at[1], group_at(z + 1, 0, 0)))
+    beside(z - 1, lambda: tell(down_sem.at[1], group_at(z - 1, 0, 0)))
+    send(group_at(z, 1, 1))
+
+    @pl.loop(1, levels, unroll=levels <= 4)
+    def _(d):
+        def reach(ready, level, onward):
+            pl.semaphore_wait(ready.at[d], 1)
+            beside(onward, lambda: tell(ready.at[d + 1], group_at(onward, 0, 0)))
+
+            @pl.when(d > 1)
+            def _():
+                send(group_at(level, 0, 0))
+
+            for da, db in ((1, 0), (0, 1), (1, 1)):
+                send(group_at(level, da, db))
+
+        beside(z - d, lambda: reach(up_sem, z - d, z + 1))
+        beside(z + d, lambda: reach(down_sem, z + d, z - 1))
 
     own_rows = pltpu.make_async_copy(outgoing.at[me], keys.at[part, me], local_sem.at[0])
     own_ids = pltpu.make_async_copy(out_ids.at[me], key_ids.at[part, me], local_sem.at[1])
@@ -147,14 +187,24 @@
     for d in range(1, parts):
         forward(me, sibling(d), d, part).start()
 
-    @pl.loop(0, groups - 1)
-    def _(t):
-        q = peer_in(t)
+    def take(q):
         row_copy(q, q).wait_recv()
         for d in range(1, parts):
             forward(q, sibling(d), d, part).start()
 
-    @pl.loop(0, groups - 1)
+    for da, db in ((1, 0), (0, 1), (1, 1)):
+        take(group_at(z, da, db))
+
+    @pl.loop(1, levels, unroll=levels <= 4)
+    def _(d):
+        def take_level(level):
+            for da, db in ((0, 0), (1, 0), (0, 1), (1, 1)):
+                take(group_at(level, da, db))
+
+        beside(z - d, lambda: take_level(z - d))
+        beside(z + d, lambda: take_level(z + d))
+
+    @pl.loop(0, groups - 1, unroll=groups <= 16)
     def _(t):
         q = peer_in(t)
         id_copy(q, q).wait_recv()
@@ -180,7 +230,7 @@
     for d in range(1, parts):
         home = sibling(d)
 
-        @pl.loop(0, groups)
+        @pl.loop(0, groups, unroll=groups <= 16)
         def _(q):
             forward(q, home, d, home).wait_recv()
 
@@ -254,7 +304,7 @@
             device_id=device(to, part), device_id_type=MESH,
         )
 
-    @pl.loop(0, groups - 1)
+    @pl.loop(0, groups - 1, unroll=groups <= 16)
     def _(t):
         ret_copy(peer_out(t), me).start()
 
@@ -262,7 +312,7 @@
     own_ret.start()
     own_ret.wait()
 
-    @pl.loop(0, groups - 1)
+    @pl.loop(0, groups - 1, unroll=groups <= 16)
     def _(t):
         q = peer_in(t)
         id_copy(q, q).wait_send()
@@ -272,20 +322,20 @@
         forward_ids(sibling(d), d, part).wait_send()
         sum_copy(sibling(d), d, part).wait_send()
 
-        @pl.loop(0, groups)
+        @pl.loop(0, groups, unroll=groups <= 16)
         def _(q):
             forward(q, sibling(d), d, part).wait_send()
 
-    @pl.loop(0, groups - 1)
+    @pl.loop(0, groups - 1, unroll=groups <= 16)
     def _(t):
         q = peer_in(t)
         ret_copy(q, q).wait_recv()
 
     back = jnp.concatenate([returned[g] for g in range(groups)], axis=0)
     picked = dot(back, lane_hit, precision=lax.Precision.HIGHEST)
-    out_ref[...] = jnp.sum(owner_hot * picked, axis=0, keepdims=True)
-
-    @pl.loop(0, groups - 1)
+    out_ref[...] = jnp.sum(owner_hot * picked, axis=0)
+
+    @pl.loop(0, groups - 1, unroll=groups <= 16)
     def _(t):
         q = peer_in(t)
         ret_copy(q, q).wait_send()
@@ -301,10 +351,12 @@
     lane_rows = slots // LANES
     local_clusters = clusters_all // groups
     dma = pltpu.SemaphoreType.DMA
+    regular = pltpu.SemaphoreType.REGULAR
+    levels = groups // PLANE
     vmem = pl.BlockSpec(memory_space=pltpu.VMEM)
     out = pl.pallas_call(
         functools.partial(kernel, groups, parts, local_clusters),
-        out_shape=jax.ShapeDtypeStruct((1, rows_here), F32),
+        out_shape=jax.ShapeDtypeStruct((rows_here,), F32),
         in_specs=[vmem] * 3,
         out_specs=vmem,
         scratch_shapes=[
@@ -321,13 +373,14 @@
             dma((groups,)), dma((groups,)), dma((groups,)), dma((groups,)),
             dma((parts, groups)), dma((parts, groups)), dma((parts,)), dma((parts,)),
             dma((parts,)), dma((parts,)), dma((groups,)), dma((groups,)), dma((3,)),
+            regular, regular((levels + 1,)), regular((levels + 1,)),
         ],
         compiler_params=pltpu.CompilerParams(
             collective_id=0, has_side_effects=True, vmem_limit_bytes=60 * 1024 * 1024
         ),
         name="soft_neighbour",
     )(embeddings, cluster_id.reshape(1, rows_here), owner_map.reshape(1, clusters_all))
-    return out.reshape(rows_here)
+    return out
 
 
 def solution(mesh):

time: 39.6 us -> 38.5 us (0.972)
  Pallas kernels: 38.2 us -> 37.1 us
    pallas_call x1, Pallas kernels: 38.2 us -> 37.1 us  [on_device(): pl.pallas_call(functools.partial(kernel, groups, parts, local_clusters),...]
    unnamed x3 -> x1, local copies, waits for them, and re-layouts: 1.22 us -> 1.24 us
where the time goes in v2:
time: 38.5 us; the launch traced here: 38.4 us
  Pallas kernels  37.1 us (96%)
  local copies, waits for them, and re-layouts  1.24 us (3%)
    pallas_call x1, Pallas kernels, on_device(): pl.pallas_call(functools.partial(kernel, groups, parts, local_clusters),...  37.1 us
    unnamed x1, local copies, waits for them, and re-layouts  1.24 us

profile of v2, /device:TPU:0, one launch (start us, length us, event | category | flops | bytes accessed | tf_op | source)
XLA Modules:
  0.0 38.4 jit_solution(219457264055498306)
XLA Ops:
  0.0 37.1 %soft_neighbour.1 = f32[256]{0:T(256)} custom-call(bf16[256,768]{1,0:T(8,128)(2,1)} %emb_ref.1, s32[1,256]{1,0:T(1,128)} %bitcast.2, s32[1,128]{1,0:T(1,128)} %bitcast.3), custom_call_target="tpu_custom_call" | custom-call | tf_op jit(solution)/shard_map/soft_neighbour/pallas_call | solution.py:357
  37.1 1.2 %copy.5 = f32[256]{0:T(256)} copy(f32[256]{0:T(256)} %soft_neighbour.1) | data formatting | bytes 2048

commit v3 on v2

--- a/solution.py
+++ b/solution.py
@@ -39,9 +39,9 @@
 def kernel(
     groups, parts, local_clusters,
     emb_ref, cid_ref, owner_ref, out_ref,
-    outgoing, out_ids, keys, key_ids, id_rows, id_cols, scores, sums, result, returned,
+    outgoing, out_ids, keys, key_ids, id_rows, id_cols, scores, result, returned,
     send_sem, recv_sem, id_send, id_recv, fwd_send, fwd_recv, idf_send, idf_recv,
-    sum_send, sum_recv, ret_send, ret_recv, local_sem, diag_sem, up_sem, down_sem,
+    ret_send, ret_recv, local_sem, diag_sem, up_sem, down_sem,
 ):
     rows_here, width = emb_ref.shape
     clusters_all = owner_ref.shape[1]
@@ -108,6 +108,8 @@
     id_block = dot(labels.astype(BF16), lane_hit.astype(BF16), ((1,), (1,)))
     for g in range(groups):
         out_ids[g] = id_block[g : g + 1]
+    label = jnp.sum(labels, axis=0, keepdims=True).astype(jnp.int32)
+    local_hit = one_hot(iota((LANES, rows_here), 0) + 1 == label, F32)
     rank_hot = one_hot(iota((cap, rows_here), 0) == rank, F32)
     emb = emb_ref[...]
     per_step = max(1, 256 // cap)
@@ -170,13 +172,29 @@
 
             @pl.when(d > 1)
             def _():
-                send(group_at(level, 0, 0))
+                id_copy(group_at(level, 0, 0), me).start()
 
             for da, db in ((1, 0), (0, 1), (1, 1)):
-                send(group_at(level, da, db))
+                id_copy(group_at(level, da, db), me).start()
+
+            @pl.when(d == 1)
+            def _():
+                row_copy(group_at(level, 1, 0), me).start()
+
+            @pl.when(d > 1)
+            def _():
+                for da, db in ((1, 1), (0, 0), (1, 0), (0, 1)):
+                    row_copy(group_at(level, da, db), me).start()
 
         beside(z - d, lambda: reach(up_sem, z - d, z + 1))
         beside(z + d, lambda: reach(down_sem, z + d, z - 1))
+
+    def send_rest(level):
+        row_copy(group_at(level, 1, 1), me).start()
+        row_copy(group_at(level, 0, 1), me).start()
+
+    beside(z - 1, lambda: send_rest(z - 1))
+    beside(z + 1, lambda: send_rest(z + 1))
 
     own_rows = pltpu.make_async_copy(outgoing.at[me], keys.at[part, me], local_sem.at[0])
     own_ids = pltpu.make_async_copy(out_ids.at[me], key_ids.at[part, me], local_sem.at[1])
@@ -194,15 +212,6 @@
 
     for da, db in ((1, 0), (0, 1), (1, 1)):
         take(group_at(z, da, db))
-
-    @pl.loop(1, levels, unroll=levels <= 4)
-    def _(d):
-        def take_level(level):
-            for da, db in ((0, 0), (1, 0), (0, 1), (1, 1)):
-                take(group_at(level, da, db))
-
-        beside(z - d, lambda: take_level(z - d))
-        beside(z + d, lambda: take_level(z + d))
 
     @pl.loop(0, groups - 1, unroll=groups <= 16)
     def _(t):
@@ -226,6 +235,15 @@
         row = id_rows[part, l]
         query_rows.append(row)
         id_cols[l * LANES : (l + 1) * LANES] = jnp.transpose(jnp.broadcast_to(row, (LANES, LANES)))
+
+    @pl.loop(1, levels, unroll=levels <= 4)
+    def _(d):
+        def take_level(level):
+            for da, db in ((0, 0), (1, 0), (0, 1), (1, 1)):
+                take(group_at(level, da, db))
+
+        beside(z - d, lambda: take_level(z - d))
+        beside(z + d, lambda: take_level(z + d))
 
     for d in range(1, parts):
         home = sibling(d)
@@ -274,41 +292,31 @@
     member = labels_row == (iota((local_clusters, slots), 0) + 1).astype(F32)
     part_sum = jnp.sum(jnp.where(member, density, 0.0), axis=1, keepdims=True)
     part_count = jnp.sum(jnp.where(member, 1.0, 0.0), axis=1, keepdims=True)
-    sums[part] = jnp.where(iota((local_clusters, LANES), 1) == 0, part_sum, part_count)
-
-    def sum_copy(piece, d, home):
+    diagonal = iota((local_clusters, LANES), 0) == iota((local_clusters, LANES), 1)
+    sum_row = jnp.sum(jnp.where(diagonal, part_sum, 0.0), axis=0, keepdims=True)
+    count_row = jnp.sum(jnp.where(diagonal, part_count, 0.0), axis=0, keepdims=True)
+    kept = jnp.where(labels_row > 0.5, density, 0.0)
+    for l in range(lane_rows):
+        result[l] = jnp.concatenate(
+            [kept[:, l * LANES : (l + 1) * LANES], sum_row, count_row, count_row], axis=0
+        )
+
+    def ret_copy(to, piece, home, frm):
         return pltpu.make_async_remote_copy(
-            src_ref=sums.at[home], dst_ref=sums.at[home],
-            send_sem=sum_send.at[d], recv_sem=sum_recv.at[home],
-            device_id=device(me, piece), device_id_type=MESH,
-        )
-
-    for d in range(1, parts):
-        sum_copy(sibling(d), d, part).start()
-    for d in range(1, parts):
-        home = sibling(d)
-        sum_copy(home, d, home).wait_recv()
-    both = sums[0]
-    for piece in range(1, parts):
-        both = both + sums[piece]
-    mean = both[:, 0:1] / jnp.maximum(both[:, 1:2], 1.0)
-    row_mean = jnp.sum(jnp.where(member, mean, 0.0), axis=0, keepdims=True)
-    final = jnp.where(labels_row > 0.5, density - row_mean, 0.0)
-    for l in range(lane_rows):
-        result[l] = final[:, l * LANES : (l + 1) * LANES]
-
-    def ret_copy(to, frm):
-        return pltpu.make_async_remote_copy(
-            src_ref=result.at[to // per_row], dst_ref=returned.at[me],
-            send_sem=ret_send.at[to], recv_sem=ret_recv.at[frm],
-            device_id=device(to, part), device_id_type=MESH,
+            src_ref=result.at[to // per_row], dst_ref=returned.at[part, me],
+            send_sem=ret_send.at[piece, to], recv_sem=ret_recv.at[home, frm],
+            device_id=device(to, piece), device_id_type=MESH,
         )
 
     @pl.loop(0, groups - 1, unroll=groups <= 16)
     def _(t):
-        ret_copy(peer_out(t), me).start()
-
-    own_ret = pltpu.make_async_copy(result.at[me // per_row], returned.at[me], local_sem.at[2])
+        for d in range(parts):
+            ret_copy(peer_out(t), sibling(d), part, me).start()
+
+    for d in range(1, parts):
+        ret_copy(me, sibling(d), part, me).start()
+
+    own_ret = pltpu.make_async_copy(result.at[me // per_row], returned.at[part, me], local_sem.at[2])
     own_ret.start()
     own_ret.wait()
 
@@ -320,7 +328,6 @@
 
     for d in range(1, parts):
         forward_ids(sibling(d), d, part).wait_send()
-        sum_copy(sibling(d), d, part).wait_send()
 
         @pl.loop(0, groups, unroll=groups <= 16)
         def _(q):
@@ -329,16 +336,34 @@
     @pl.loop(0, groups - 1, unroll=groups <= 16)
     def _(t):
         q = peer_in(t)
-        ret_copy(q, q).wait_recv()
-
-    back = jnp.concatenate([returned[g] for g in range(groups)], axis=0)
-    picked = dot(back, lane_hit, precision=lax.Precision.HIGHEST)
+        for d in range(parts):
+            ret_copy(q, sibling(d), sibling(d), q).wait_recv()
+
+    for d in range(1, parts):
+        ret_copy(me, sibling(d), sibling(d), me).wait_recv()
+
+    back = jnp.concatenate([returned[part, g, 0:1] for g in range(groups)], axis=0)
+    total_sum = jnp.concatenate([returned[0, g, 1:2] for g in range(groups)], axis=0)
+    total_count = jnp.concatenate([returned[0, g, 2:3] for g in range(groups)], axis=0)
+    for piece in range(1, parts):
+        total_sum += jnp.concatenate([returned[piece, g, 1:2] for g in range(groups)], axis=0)
+        total_count += jnp.concatenate([returned[piece, g, 2:3] for g in range(groups)], axis=0)
+    mean = total_sum / jnp.maximum(total_count, 1.0)
+    picked = dot(
+        jnp.concatenate([back, -mean], axis=1),
+        jnp.concatenate([lane_hit, local_hit], axis=0),
+        precision=lax.Precision.HIGHEST,
+    )
     out_ref[...] = jnp.sum(owner_hot * picked, axis=0)
 
     @pl.loop(0, groups - 1, unroll=groups <= 16)
     def _(t):
         q = peer_in(t)
-        ret_copy(q, q).wait_send()
+        for d in range(parts):
+            ret_copy(q, sibling(d), sibling(d), q).wait_send()
+
+    for d in range(1, parts):
+        ret_copy(me, sibling(d), sibling(d), me).wait_send()
 
 
 def on_device(embeddings, cluster_id, owner_map):
@@ -367,12 +392,11 @@
             pltpu.VMEM((parts, lane_rows, 1, LANES), F32),
             pltpu.VMEM((slots, LANES), F32),
             pltpu.VMEM((parts * slots // KEY_CHUNK, slots, KEY_CHUNK), F32),
-            pltpu.VMEM((parts, local_clusters, LANES), F32),
-            pltpu.VMEM((lane_rows, 1, LANES), F32),
-            pltpu.VMEM((groups, 1, LANES), F32),
+            pltpu.VMEM((lane_rows, 4, LANES), F32),
+            pltpu.VMEM((parts, groups, 4, LANES), F32),
             dma((groups,)), dma((groups,)), dma((groups,)), dma((groups,)),
             dma((parts, groups)), dma((parts, groups)), dma((parts,)), dma((parts,)),
-            dma((parts,)), dma((parts,)), dma((groups,)), dma((groups,)), dma((3,)),
+            dma((parts, groups)), dma((parts, groups)), dma((3,)),
             regular, regular((levels + 1,)), regular((levels + 1,)),
         ],
         compiler_params=pltpu.CompilerParams(

time: 38.5 us -> 37.2 us (0.966)
  Pallas kernels: 37.1 us -> 35.8 us
    pallas_call x1, Pallas kernels: 37.1 us -> 35.8 us  [on_device(): pl.pallas_call(functools.partial(kernel, groups, parts, local_clusters),...]
where the time goes in v3:
time: 37.2 us; the launch traced here: 37 us
  Pallas kernels  35.8 us (96%)
  local copies, waits for them, and re-layouts  1.24 us (3%)
    pallas_call x1, Pallas kernels, on_device(): pl.pallas_call(functools.partial(kernel, groups, parts, local_clusters),...  35.8 us
    unnamed x1, local copies, waits for them, and re-layouts  1.24 us

profile of v3, /device:TPU:0, one launch (start us, length us, event | category | flops | bytes accessed | tf_op | source)
XLA Modules:
  0.0 37.0 jit_solution(7447058801822084312)
XLA Ops:
  0.0 35.8 %soft_neighbour.1 = f32[256]{0:T(256)} custom-call(bf16[256,768]{1,0:T(8,128)(2,1)} %emb_ref.1, s32[1,256]{1,0:T(1,128)} %bitcast.2, s32[1,128]{1,0:T(1,128)} %bitcast.3), custom_call_target="tpu_custom_call" | custom-call | tf_op jit(solution)/shard_map/soft_neighbour/pallas_call | solution.py:382
  35.8 1.2 %copy.5 = f32[256]{0:T(256)} copy(f32[256]{0:T(256)} %soft_neighbour.1) | data formatting | bytes 2048

commit v4 on v3

--- a/solution.py
+++ b/solution.py
@@ -38,10 +38,11 @@
 
 def kernel(
     groups, parts, local_clusters,
-    emb_ref, cid_ref, owner_ref, out_ref,
+    emb_in, cid_in, owner_in, out_ref,
+    emb_ref, cid_ref, owner_ref,
     outgoing, out_ids, keys, key_ids, id_rows, id_cols, scores, result, returned,
     send_sem, recv_sem, id_send, id_recv, fwd_send, fwd_recv, idf_send, idf_recv,
-    ret_send, ret_recv, local_sem, diag_sem, up_sem, down_sem,
+    ret_send, ret_recv, local_sem, diag_sem, up_sem, down_sem, load_sem,
 ):
     rows_here, width = emb_ref.shape
     clusters_all = owner_ref.shape[1]
@@ -91,6 +92,15 @@
     beside(z + 1, lambda: tell(barrier, group_at(z + 1, 0, 0)))
     for d in range(1, parts):
         pl.semaphore_signal(barrier, inc=1, device_id=device(me, sibling(d)), device_id_type=MESH)
+
+    loads = [
+        pltpu.make_async_copy(given, held, load_sem.at[i])
+        for i, (given, held) in enumerate(((cid_in, cid_ref), (owner_in, owner_ref), (emb_in, emb_ref)))
+    ]
+    for load in loads:
+        load.start()
+    loads[0].wait()
+    loads[1].wait()
 
     cid = cid_ref[...]
     cluster_hit = one_hot(iota((clusters_all, rows_here), 0) == cid)
@@ -111,6 +121,7 @@
     label = jnp.sum(labels, axis=0, keepdims=True).astype(jnp.int32)
     local_hit = one_hot(iota((LANES, rows_here), 0) + 1 == label, F32)
     rank_hot = one_hot(iota((cap, rows_here), 0) == rank, F32)
+    loads[2].wait()
     emb = emb_ref[...]
     per_step = max(1, 256 // cap)
     for g0 in range(0, groups, per_step):
@@ -382,9 +393,12 @@
     out = pl.pallas_call(
         functools.partial(kernel, groups, parts, local_clusters),
         out_shape=jax.ShapeDtypeStruct((rows_here,), F32),
-        in_specs=[vmem] * 3,
+        in_specs=[pl.BlockSpec(memory_space=pl.ANY)] * 3,
         out_specs=vmem,
         scratch_shapes=[
+            pltpu.VMEM((rows_here, width), BF16),
+            pltpu.VMEM((1, rows_here), jnp.int32),
+            pltpu.VMEM((1, clusters_all), jnp.int32),
             pltpu.VMEM((groups, cap, width), BF16),
             pltpu.VMEM((groups, 1, LANES), F32),
             pltpu.VMEM((parts, groups, cap, width), BF16),
@@ -397,7 +411,7 @@
             dma((groups,)), dma((groups,)), dma((groups,)), dma((groups,)),
             dma((parts, groups)), dma((parts, groups)), dma((parts,)), dma((parts,)),
             dma((parts, groups)), dma((parts, groups)), dma((3,)),
-            regular, regular((levels + 1,)), regular((levels + 1,)),
+            regular, regular((levels + 1,)), regular((levels + 1,)), dma((3,)),
         ],
         compiler_params=pltpu.CompilerParams(
             collective_id=0, has_side_effects=True, vmem_limit_bytes=60 * 1024 * 1024

time: 37.2 us -> 36.5 us (0.981)
  Pallas kernels: 35.8 us -> 35.1 us
    pallas_call x1, Pallas kernels: 35.8 us -> 35.1 us  [on_device(): pl.pallas_call(functools.partial(kernel, groups, parts, local_clusters),...]
where the time goes in v4:
time: 36.5 us; the launch traced here: 36.4 us
  Pallas kernels  35.1 us (96%)
  local copies, waits for them, and re-layouts  1.24 us (3%)
    pallas_call x1, Pallas kernels, on_device(): pl.pallas_call(functools.partial(kernel, groups, parts, local_clusters),...  35.1 us
    unnamed x1, local copies, waits for them, and re-layouts  1.24 us

profile of v4, /device:TPU:0, one launch (start us, length us, event | category | flops | bytes accessed | tf_op | source)
XLA Modules:
  0.0 36.4 jit_solution(18343402653563469304)
XLA Ops:
  0.0 35.1 %soft_neighbour.1 = f32[256]{0:T(256)} custom-call(bf16[256,768]{1,0:T(8,128)(2,1)} %emb_in.1, s32[1,256]{1,0:T(1,128)} %bitcast.2, s32[1,128]{1,0:T(1,128)} %bitcast.3), custom_call_target="tpu_custom_call" | custom-call | tf_op jit(solution)/shard_map/soft_neighbour/pallas_call | solution.py:393
  35.1 1.2 %copy.5 = f32[256]{0:T(256)} copy(f32[256]{0:T(256)} %soft_neighbour.1) | data formatting | bytes 2048
